TPU v7x, 32 devices: a whole 2x2x4 slice. The times are simulated.
32 devices in a mesh: gx: 4 (over x, core), gy: 8 (over z, y).
Axes of the slice: x: 2, y: 2, z: 4, core: 2. Of those that a mesh axis runs over, the one named last changes fastest.
Arguments:
- field: float32 [12, 64, 64, 128], P(None, 'gx', 'gy'), may hold values from -16 to 16
- diffusion: float32 [12], replicated, may hold values from 0.02 to 0.15
- prefactor: float32 [12], replicated, may hold values from 0.05 to 0.3
- activation: float32 [12], replicated, may hold values from 0.5 to 2
- mixing: float32 [12, 12], replicated, may hold values from -1.75 to 1.75
- basis_x: float32 [64, 64], P('gx'), may hold values from -1 to 1, as said below
- basis_y: float32 [64, 64], P('gy'), may hold values from -1 to 1, as said below
- basis_z: float32 [128, 32], replicated, may hold values from -1 to 1, as said below
- basis_v: float32 [12, 6], replicated, may hold values from -1 to 1, as said below
Outputs:
- state: float32 [12, 64, 64, 128], P(None, 'gx', 'gy')
- recon: float32 [12, 64, 64, 128], P(None, 'gx', 'gy')
- residual: float32 [12], replicated
Inputs may be any that keep to these rules, and one draw needn't show every extreme that they name: `basis_x`: its 64 columns are mutually orthogonal, each of norm between 0.5 and 1. `basis_y`: its 64 columns are orthonormal. `basis_z`: its 32 columns are orthonormal. `basis_v`: its 6 columns are orthonormal.
All inputs are finite; a program needn't handle non-finite values.
Results may differ from a plain program's by a relative error of at most 0.00013.
Values sent between devices are 32-bit elements; how exact they have to be, the bound alone decides.
No kernel may reach another device: no remote copies, remote signals or barrier semaphores. Data moves between devices by JAX's collectives and lax.ppermute only.
A program may use at most 64 MiB of HBM per device.

v0:
```python
import jax
import jax.numpy as jnp
from jax import lax
from jax.sharding import PartitionSpec as P

HIGH = lax.Precision.HIGHEST


def padded_2(array, sides, width):
    for axis, dim in sides:
        peers, length = (lax.axis_size(axis), array.shape[dim])
        up = [(i, (i + 1) % peers) for i in range(peers - 1)]
        down = [(j, i) for i, j in up]
        last = lax.slice_in_dim(array, length - width, length, axis=dim)
        first = lax.slice_in_dim(array, 0, width, axis=dim)
        before = lax.ppermute(last, axis, up)
        after = lax.ppermute(first, axis, down)
        array = jnp.concatenate([before, array, after], axis=dim)
    return array


def lap_core(padded):
    centre = padded[:, 1:-1, 1:-1, 1:-1]
    summed = padded[:, 2:, 1:-1, 1:-1] + padded[:, :-2, 1:-1, 1:-1]
    summed = summed + padded[:, 1:-1, 2:, 1:-1] + padded[:, 1:-1, :-2, 1:-1]
    summed = summed + padded[:, 1:-1, 1:-1, 2:] + padded[:, 1:-1, 1:-1, :-2]
    return summed - 6.0 * centre


def reaction(centre, coeffs):
    diffusion, prefactor, activation, mixing = coeffs
    temper = 1.5 + jnp.tanh(centre[0])
    rate_terms = (
        prefactor[:, None, None, None]
        * jnp.exp(-activation[:, None, None, None] / temper[None])
        * centre
    )
    return jnp.einsum("vw,wxyz->vxyz", mixing, rate_terms, precision=HIGH)


def tendency(rimmed, centre, coeffs):
    padded = jnp.pad(rimmed, ((0, 0), (0, 0), (0, 0), (1, 1)))
    return coeffs[0][:, None, None, None] * lap_core(padded) + reaction(centre, coeffs)


def inside_mask(rows_x, rows_y):
    pos_x = lax.axis_index("gx") * rows_x + jnp.arange(rows_x + 2) - 1
    pos_y = lax.axis_index("gy") * rows_y + jnp.arange(rows_y + 2) - 1
    in_x = (pos_x >= 0) & (pos_x < rows_x * lax.axis_size("gx"))
    in_y = (pos_y >= 0) & (pos_y < rows_y * lax.axis_size("gy"))
    return in_x[:, None] & in_y[None, :]


def step_deep(state, coeffs, inside):
    wide = padded_2(state, (("gx", 1), ("gy", 2)), 2)
    centre = wide[:, 1:-1, 1:-1]
    section_wide = centre + tendency(wide, centre, coeffs)
    section_wide = jnp.where(inside[None, :, :, None], section_wide, 0.0)
    section = section_wide[:, 1:-1, 1:-1]
    return 0.5 * (state + section + tendency(section_wide, section, coeffs))


def on_device(field, diffusion, prefactor, activation, mixing, basis_x, basis_y, basis_z, basis_v):
    coeffs = (diffusion, prefactor, activation, mixing)
    rows_x = field.shape[1]
    rows_y = field.shape[2]
    state = field
    inside = inside_mask(rows_x, rows_y)
    state = step_deep(state, coeffs, inside)
    rank_z = basis_z.shape[1]
    rank_v = basis_v.shape[1]
    width = rank_z * rank_v
    proj_z = jnp.einsum("vxyz,zr->vxyr", state, basis_z, precision=HIGH)
    packed = jnp.einsum("vxyr,vs->xyrs", proj_z, basis_v, precision=HIGH)
    packed = packed.reshape(rows_x, rows_y, width)
    columns = basis_x
    part_x = lax.psum_scatter(
        jnp.einsum("xa,xyk->ayk", columns, packed, precision=HIGH),
        "gx",
        scatter_dimension=0,
        tiled=True,
    )
    core_block = jnp.einsum("ayk,yb->abk", part_x, basis_y, precision=HIGH)
    core_block = lax.psum(core_block, "gy")
    mixed_y = jnp.einsum("abk,yb->ayk", core_block, basis_y, precision=HIGH)
    columns = basis_x
    decoded = jnp.einsum(
        "xa,ayk->xyk", columns, lax.all_gather(mixed_y, "gx", axis=0, tiled=True), precision=HIGH
    )
    decoded = decoded.reshape(rows_x, rows_y, rank_z, rank_v)
    back_v = jnp.einsum("xyrs,vs->vxyr", decoded, basis_v, precision=HIGH)
    recon = jnp.einsum("vxyr,zr->vxyz", back_v, basis_z, precision=HIGH)
    error = state - recon
    miss_local = jnp.sum(error * error, axis=(1, 2, 3))
    mass_local = jnp.sum(state * state, axis=(1, 2, 3))
    miss, mass = lax.psum((miss_local, mass_local), ("gx", "gy"))
    residual = jnp.sqrt(miss / (mass + 1e-06))
    return (state, recon, residual)


def solution(mesh):
    return jax.shard_map(
        on_device,
        mesh=mesh,
        in_specs=(
            P(None, "gx", "gy", None),
            P(),
            P(),
            P(),
            P(),
            P("gx", None),
            P("gy", None),
            P(),
            P(),
        ),
        out_specs=(P(None, "gx", "gy", None), P(None, "gx", "gy", None), P()),
        check_vma=False,
    )
```

profile of v0, /device:TPU:0, one launch (start us, length us, event | category | flops | bytes accessed | tf_op | source)
XLA Modules:
  0.0 209.1 jit_solution(7740615977400366910)
XLA Ops:
  7.2 0.0 copy-start
  7.2 0.0 reduce-scatter.2.cloned.1.call-start
  7.2 1.0 fusion.57
  8.3 2.4 %collective-permute-start = (f32[12,2,8,128]{3,0,2,1:T(8,128)S(1)}, f32[12,2,8,128]{3,0,2,1:T(8,128)S(1)}, u32[]{:S(2)}, u32[]{:S(2)}) collective-permute-start(f32[12,2,8,128]{3,0,2,1:T(8,128)S(1)} %copy.76), channel_id=1, source_target_pairs={{0,8},{8,16},{16,24},{1,9},{9,17},{17,25},{2,10},{10,18},{18,26},{... | collective-permute-start | bytes 294920 | tf_op jit(solution)/shard_map/ppermute | solution.py:16
  10.8 1.3 collective-permute-start.1
  12.1 0.0 collective-permute-done
  12.1 0.0 copy-start.7
  12.1 0.5 copy_dynamic-update-slice_fusion
  12.6 3.5 %collective-permute-done.1 = f32[12,2,8,128]{3,0,2,1:T(8,128)S(1)} collective-permute-done((f32[12,2,8,128]{3,0,2,1:T(8,128)S(1)}, f32[12,2,8,128]{3,0,2,1:T(8,128)S(1)}, u32[]{:S(2)}, u32[]{:S(2)}) %collective-permute-start.1) | collective-permute-done | bytes 98336 | tf_op jit(solution)/shard_map/ppermute | solution.py:17
  16.2 3.4 %collective-permute-start.2 = (f32[12,20,2,128]{3,0,2,1:T(8,128)S(1)}, f32[12,20,2,128]{3,0,2,1:T(8,128)S(1)}, u32[]{:S(2)}, u32[]{:S(2)}) collective-permute-start(f32[12,20,2,128]{3,0,2,1:T(8,128)S(1)} %get-tuple-element.19), channel_id=1, source_target_pairs={{0,1},{1,2},{2,3},{3,4},{4,5},{5,6},{6,7},{8,9},{9,10},{10,11},{11... | collective-permute-start | bytes 737288 | tf_op jit(solution)/shard_map/ppermute | solution.py:16
  19.6 1.3 collective-permute-start.3
  20.9 0.0 copy-done.7
  20.9 0.1 broadcast_and_fusion
  21.0 4.2 %collective-permute-done.2 = f32[12,20,2,128]{3,0,2,1:T(8,128)S(1)} collective-permute-done((f32[12,20,2,128]{3,0,2,1:T(8,128)S(1)}, f32[12,20,2,128]{3,0,2,1:T(8,128)S(1)}, u32[]{:S(2)}, u32[]{:S(2)}) %collective-permute-start.2) | collective-permute-done | bytes 245792 | tf_op jit(solution)/shard_map/ppermute | solution.py:16
  25.2 4.6 %collective-permute-done.3 = f32[12,20,2,128]{3,0,2,1:T(8,128)S(1)} collective-permute-done((f32[12,20,2,128]{3,0,2,1:T(8,128)S(1)}, f32[12,20,2,128]{3,0,2,1:T(8,128)S(1)}, u32[]{:S(2)}, u32[]{:S(2)}) %collective-permute-start.3) | collective-permute-done | bytes 245792 | tf_op jit(solution)/shard_map/ppermute | solution.py:17
  29.8 0.2 pad_maximum_fusion
  30.0 0.1 fusion.41
  30.1 2.3 %fusion.8 = f32[12,18,10,128]{3,0,2,1:T(8,128)S(1)} fusion(f32[12,20,12,128]{3,0,2,1:T(8,128)S(1)} %pad_maximum_fusion, f32[12,20,8,128]{3,0,2,1:T(8,128)S(1)} %constant_dynamic-update-slice_fusion, f32[12,20,2,128]{3,0,2,1:T(8,128)S(1)} %collective-permute-done.2, f32[12,20,2,128]{3,0,2,1:T(8,128)S(1)} %collective-permute-done.3, ...), kind=kOutput, calls=%fused_computation.14 | convolution fusion | flops 44236800 | bytes 11096576 | tf_op jit(solution)/shard_map/vw,wxyz->vxyz/dot_general | solution.py:38
  32.5 0.1 fusion.42
  32.6 2.2 %fusion.23 = f32[12,16,8,128]{3,0,2,1:T(8,128)S(1)} fusion(f32[12,18,10,128]{3,0,2,1:T(8,128)S(1)} %fusion.8, f32[16,8,128]{2,1,0:T(8,128)S(1)} %bitcast.62, f32[12]{0:T(128)S(1)} %neg.5, f32[12]{0:T(128)S(1)} %copy-done.8, f32[12]{0:T(128)S(1)} %copy-done.9, f32[12,16,8,128]{3,2,1,0:T(8,128)S(1)} %copy-done.2, f32[12,12]{1,0:T(8,128)S(1)} %copy-done.6), kind=kOutput, calls=%fused_computation.37 | convolution fusion | flops 31260672 | bytes 9414144 | tf_op jit(solution)/shard_map/vw,wxyz->vxyz/dot_general | solution.py:38
  34.8 0.0 copy-start.5
  34.8 1.0 fusion.44
  35.8 0.0 copy-done.5
  35.8 0.0 copy-start.3
  35.8 0.7 fusion.51
  36.5 0.5 copy.49
  37.1 0.0 copy-start.4
  37.1 1.7 convolution_bitcast_fusion.3
  38.7 1.1 copy.51
  39.8 0.0 reduce-scatter.2.cloned.1.call-update
  39.9 0.0 all-reduce.5.cloned.1.call-start
  39.9 27.8 %reduce-scatter.2.cloned.1.call-done = f32[16,8,192]{2,1,0:T(8,128)} async-done(((f32[64,8,192]{2,1,0:T(8,128)}), f32[16,8,192]{2,1,0:T(8,128)}) %reduce-scatter.2.cloned.1.call-update) | async-done | bytes 98320 | tf_op jit(solution)/shard_map/reduce_scatter | solution.py:77
  67.7 0.0 copy-done.4
  67.7 2.9 %convolution_bitcast_fusion.1 = f32[16,64,192]{2,1,0:T(8,128)} fusion(f32[16,8,192]{2,1,0:T(8,128)} %reduce-scatter.2.cloned.1.call-done, f32[8,64]{1,0:T(8,128)S(1)} %copy-done.4), kind=kOutput, calls=%fused_computation.23 | convolution fusion | flops 18874368 | bytes 886784 | tf_op jit(solution)/shard_map/ayk,yb->abk/dot_general | solution.py:83
  70.6 0.0 all-reduce.5.cloned.1.call-update
  70.6 1.1 copy.57
  71.7 77.8 %all-reduce.5.cloned.1.call-done = f32[16,64,192]{2,1,0:T(8,128)} async-done(((f32[16,64,192]{2,1,0:T(8,128)}), f32[16,64,192]{2,1,0:T(8,128)}) %all-reduce.5.cloned.1.call-update) | async-done | bytes 786448 | tf_op jit(solution)/shard_map/psum | solution.py:84
  149.5 1.9 convolution_bitcast_fusion.5
  151.3 7.3 %all_gather.3 = f32[64,8,192]{2,1,0:T(8,128)S(1)} all-gather(f32[16,8,192]{2,1,0:T(8,128)S(1)} %convolution_bitcast_fusion.5), channel_id=1, replica_groups=mesh['gx'=4,'gy'=8] {'gx'}, dimensions={0}, use_global_device_ids=true | all-gather | bytes 491520 | tf_op jit(solution)/shard_map/all_gather | solution.py:88
  158.7 0.5 convolution_bitcast_fusion.4
  159.2 0.3 copy.53
  159.5 0.6 copy.54
  160.1 1.0 convolution_bitcast_fusion
  161.2 0.9 fusion.31
  162.1 0.0 copy-start.1
  162.1 0.7 multiply_reduce_fusion
  162.8 38.9 %all-reduce.2 = (f32[12]{0:T(128)S(1)}, f32[12]{0:T(128)S(1)}) all-reduce(f32[12]{0:T(128)S(1)} %get-tuple-element.16, f32[12]{0:T(128)S(1)} %get-tuple-element.15), channel_id=1, replica_groups=mesh['gx'=4,'gy'=8] {'gx','gy'}, use_global_device_ids=true, to_apply=%region_3.4 | all-reduce | flops 24 | bytes 192 | tf_op jit(solution)/shard_map/psum | solution.py:96
  201.7 0.5 fusion.55
  (20 shorter events, 0.2 us)
Async XLA Ops:
  7.2 27.6 %copy-start = (f32[128,32]{0,1:T(8,128)S(1)}, f32[128,32]{0,1:T(8,128)}, u32[]{:S(2)}) copy-start(f32[128,32]{0,1:T(8,128)} %param.16) | copy-start | bytes 49156
  7.2 4.9 %copy-start.2 = (f32[12,16,8,128]{3,2,1,0:T(8,128)S(1)}, f32[12,16,8,128]{3,2,1,0:T(8,128)}, u32[]{:S(2)}) copy-start(f32[12,16,8,128]{3,2,1,0:T(8,128)} %param.9) | copy-start | bytes 2359300
  7.2 60.5 %reduce-scatter.2.cloned.1.call-start = ((), (), s32[]{:S(2)}) async-start(), calls=%async_computation.1 | async-start | bytes 655360 | tf_op jit(solution)/shard_map/reduce_scatter | solution.py:77
  8.3 3.8 %collective-permute-start = (f32[12,2,8,128]{3,0,2,1:T(8,128)S(1)}, f32[12,2,8,128]{3,0,2,1:T(8,128)S(1)}, u32[]{:S(2)}, u32[]{:S(2)}) collective-permute-start(f32[12,2,8,128]{3,0,2,1:T(8,128)S(1)} %copy.76), channel_id=1, source_target_pairs={{0,8},{8,16},{16,24},{1,9},{9,17},{17,25},{2,10},{10,18},{18,26},{... | collective-permute-start | bytes 294920 | tf_op jit(solution)/shard_map/ppermute | solution.py:16
  10.8 5.3 %collective-permute-start.1 = (f32[12,2,8,128]{3,0,2,1:T(8,128)S(1)}, f32[12,2,8,128]{3,0,2,1:T(8,128)S(1)}, u32[]{:S(2)}, u32[]{:S(2)}) collective-permute-start(f32[12,2,8,128]{3,0,2,1:T(8,128)S(1)} %copy.77), channel_id=1, source_target_pairs={{8,0},{16,8},{24,16},{9,1},{17,9},{25,17},{10,2},{18,10},{26,18},{... | collective-permute-start | bytes 294920 | tf_op jit(solution)/shard_map/ppermute | solution.py:17
  12.1 8.8 %copy-start.7 = (f32[12]{0:T(128)S(1)}, f32[12]{0:T(128)}, u32[]{:S(2)}) copy-start(f32[12]{0:T(128)} %param.12) | copy-start | bytes 148
  16.2 9.0 %collective-permute-start.2 = (f32[12,20,2,128]{3,0,2,1:T(8,128)S(1)}, f32[12,20,2,128]{3,0,2,1:T(8,128)S(1)}, u32[]{:S(2)}, u32[]{:S(2)}) collective-permute-start(f32[12,20,2,128]{3,0,2,1:T(8,128)S(1)} %get-tuple-element.19), channel_id=1, source_target_pairs={{0,1},{1,2},{2,3},{3,4},{4,5},{5,6},{6,7},{8,9},{9,10},{10,11},{11... | collective-permute-start | bytes 737288 | tf_op jit(solution)/shard_map/ppermute | solution.py:16
  19.6 10.2 %collective-permute-start.3 = (f32[12,20,2,128]{3,0,2,1:T(8,128)S(1)}, f32[12,20,2,128]{3,0,2,1:T(8,128)S(1)}, u32[]{:S(2)}, u32[]{:S(2)}) collective-permute-start(f32[12,20,2,128]{3,0,2,1:T(8,128)S(1)} %get-tuple-element.20), channel_id=1, source_target_pairs={{1,0},{2,1},{3,2},{4,3},{5,4},{6,5},{7,6},{9,8},{10,9},{11,10},{12... | collective-permute-start | bytes 737288 | tf_op jit(solution)/shard_map/ppermute | solution.py:17
  21.0 9.1 %copy-start.6 = (f32[12,12]{1,0:T(8,128)S(1)}, f32[12,12]{1,0:T(8,128)}, u32[]{:S(2)}) copy-start(f32[12,12]{1,0:T(8,128)} %param.13) | copy-start | bytes 1732
  21.0 9.1 %copy-start.8 = (f32[12]{0:T(128)S(1)}, f32[12]{0:T(128)}, u32[]{:S(2)}) copy-start(f32[12]{0:T(128)} %param.11) | copy-start | bytes 148
  21.0 9.1 %copy-start.9 = (f32[12]{0:T(128)S(1)}, f32[12]{0:T(128)}, u32[]{:S(2)}) copy-start(f32[12]{0:T(128)} %param.10) | copy-start | bytes 148
  34.8 1.0 copy-start.5
  35.8 1.3 copy-start.3
  37.1 30.6 %copy-start.4 = (f32[8,64]{1,0:T(8,128)S(1)}, f32[8,64]{1,0:T(8,128)}, u32[]{:S(2)}) copy-start(f32[8,64]{1,0:T(8,128)} %param.15) | copy-start | bytes 6148
  39.9 109.6 %all-reduce.5.cloned.1.call-start = ((), (), s32[]{:S(2)}) async-start(), calls=%async_computation.2 | async-start | bytes 2097152 | tf_op jit(solution)/shard_map/psum | solution.py:84
  162.1 40.1 %copy-start.1 = (f32[12,16,8,128]{3,2,1,0:T(8,128)}, f32[12,16,8,128]{3,2,1,0:T(8,128)S(1)}, u32[]{:S(2)}) copy-start(f32[12,16,8,128]{3,2,1,0:T(8,128)S(1)} %fusion.31) | copy-start | bytes 2359300
Sparse Core Ops, SparseCore 0:
  40.0 27.6 reduce-scatter.1
  71.2 78.2 all-reduce.4
where the time goes:
time: 209 us
  waiting for transfers between devices  118 us (56%)
  blocking collectives  46.3 us (22%)
  matrix products  15.1 us (7%)
  between operations  14.4 us (7%)
  starting transfers between devices  8.51 us (4%)
  local copies, waits for them, and re-layouts  5.35 us (3%)
    psum x1, waiting for transfers between devices, on_device(): core_block = lax.psum(core_block, 'gy')  77.8 us
    psum x1, blocking collectives, on_device(): miss, mass = lax.psum((miss_local, mass_local), ('gx', 'gy'))  38.9 us
    reduce_scatter x1, waiting for transfers between devices, on_device(): lax.psum_scatter(jnp.einsum('xa,xyk->ayk', columns, packed, precision=HIG...  27.8 us
    ppermute x2, waiting for transfers between devices, padded_2(): after = lax.ppermute(first, axis, down)  8.07 us
    all_gather x1, blocking collectives, on_device(): lax.all_gather(mixed_y, 'gx', axis=0, tiled=True)  7.32 us
    ppermute x2, starting transfers between devices, padded_2(): before = lax.ppermute(last, axis, up)  5.85 us
    dot_general x2, matrix products, reaction(): return jnp.einsum('vw,wxyz->vxyz', mixing, rate_terms, precision=HIGH)  4.55 us
  transfers between devices with their start and end apart: 6, of which 5 were waited for; matrix products, arithmetic and copies ran while one was open for 1% of the time, Pallas kernels for 0%

commit v1 on v0

--- a/solution.py
+++ b/solution.py
@@ -1,9 +1,19 @@
+import functools
 import jax
 import jax.numpy as jnp
 from jax import lax
 from jax.sharding import PartitionSpec as P
 
 HIGH = lax.Precision.HIGHEST
+
+
+def end_the_groups(here_x, mesh_dim, a_name):
+    for pp in (mesh_dim, a_name):
+        here_x = lax.psum(here_x, pp)
+    return here_x
+
+
+detail_the_waves = functools.partial(end_the_groups, mesh_dim="gy", a_name="gx")
 
 
 def padded_2(array, sides, width):
@@ -93,7 +103,7 @@
     error = state - recon
     miss_local = jnp.sum(error * error, axis=(1, 2, 3))
     mass_local = jnp.sum(state * state, axis=(1, 2, 3))
-    miss, mass = lax.psum((miss_local, mass_local), ("gx", "gy"))
+    miss, mass = detail_the_waves((miss_local, mass_local))
     residual = jnp.sqrt(miss / (mass + 1e-06))
     return (state, recon, residual)
 

time: 209 us -> 196 us (0.938)
  blocking collectives: 46.3 us -> 33 us
    psum x1 -> x2, blocking collectives: 38.9 us -> 25.7 us  [end_the_groups(): here_x = lax.psum(here_x, pp)]
where the time goes in v1:
time: 196 us
  waiting for transfers between devices  118 us (60%)
  blocking collectives  33 us (17%)
  matrix products  15.1 us (8%)
  between operations  14.4 us (7%)
  starting transfers between devices  8.51 us (4%)
  local copies, waits for them, and re-layouts  5.35 us (3%)
    psum x1, waiting for transfers between devices, on_device(): core_block = lax.psum(core_block, 'gy')  77.8 us
    reduce_scatter x1, waiting for transfers between devices, on_device(): lax.psum_scatter(jnp.einsum('xa,xyk->ayk', columns, packed, precision=HIG...  27.8 us
    psum x2, blocking collectives, end_the_groups(): here_x = lax.psum(here_x, pp)  25.7 us
    ppermute x2, waiting for transfers between devices, padded_2(): after = lax.ppermute(first, axis, down)  8.07 us
    all_gather x1, blocking collectives, on_device(): lax.all_gather(mixed_y, 'gx', axis=0, tiled=True)  7.32 us
    ppermute x2, starting transfers between devices, padded_2(): before = lax.ppermute(last, axis, up)  5.85 us
    dot_general x2, matrix products, reaction(): return jnp.einsum('vw,wxyz->vxyz', mixing, rate_terms, precision=HIGH)  4.55 us
    ppermute x2, waiting for transfers between devices, padded_2(): before = lax.ppermute(last, axis, up)  4.17 us
  transfers between devices with their start and end apart: 6, of which 5 were waited for; matrix products, arithmetic and copies ran while one was open for 1% of the time, Pallas kernels for 0%

profile of v1, /device:TPU:0, one launch (start us, length us, event | category | flops | bytes accessed | tf_op | source)
XLA Modules:
  0.0 195.8 jit_solution(8393898822845535089)
XLA Ops:
  7.2 0.0 copy-start
  7.2 0.0 reduce-scatter.2.cloned.1.call-start
  7.2 1.0 fusion.57
  8.3 2.4 %collective-permute-start = (f32[12,2,8,128]{3,0,2,1:T(8,128)S(1)}, f32[12,2,8,128]{3,0,2,1:T(8,128)S(1)}, u32[]{:S(2)}, u32[]{:S(2)}) collective-permute-start(f32[12,2,8,128]{3,0,2,1:T(8,128)S(1)} %copy.76), channel_id=1, source_target_pairs={{0,8},{8,16},{16,24},{1,9},{9,17},{17,25},{2,10},{10,18},{18,26},{... | collective-permute-start | bytes 294920 | tf_op jit(solution)/shard_map/ppermute | solution.py:26
  10.8 1.3 collective-permute-start.1
  12.1 0.0 collective-permute-done
  12.1 0.0 copy-start.7
  12.1 0.5 copy_dynamic-update-slice_fusion
  12.6 3.5 %collective-permute-done.1 = f32[12,2,8,128]{3,0,2,1:T(8,128)S(1)} collective-permute-done((f32[12,2,8,128]{3,0,2,1:T(8,128)S(1)}, f32[12,2,8,128]{3,0,2,1:T(8,128)S(1)}, u32[]{:S(2)}, u32[]{:S(2)}) %collective-permute-start.1) | collective-permute-done | bytes 98336 | tf_op jit(solution)/shard_map/ppermute | solution.py:27
  16.2 3.4 %collective-permute-start.2 = (f32[12,20,2,128]{3,0,2,1:T(8,128)S(1)}, f32[12,20,2,128]{3,0,2,1:T(8,128)S(1)}, u32[]{:S(2)}, u32[]{:S(2)}) collective-permute-start(f32[12,20,2,128]{3,0,2,1:T(8,128)S(1)} %get-tuple-element.21), channel_id=1, source_target_pairs={{0,1},{1,2},{2,3},{3,4},{4,5},{5,6},{6,7},{8,9},{9,10},{10,11},{11... | collective-permute-start | bytes 737288 | tf_op jit(solution)/shard_map/ppermute | solution.py:26
  19.6 1.3 collective-permute-start.3
  20.9 0.0 copy-done.7
  20.9 0.1 broadcast_and_fusion
  21.0 4.2 %collective-permute-done.2 = f32[12,20,2,128]{3,0,2,1:T(8,128)S(1)} collective-permute-done((f32[12,20,2,128]{3,0,2,1:T(8,128)S(1)}, f32[12,20,2,128]{3,0,2,1:T(8,128)S(1)}, u32[]{:S(2)}, u32[]{:S(2)}) %collective-permute-start.2) | collective-permute-done | bytes 245792 | tf_op jit(solution)/shard_map/ppermute | solution.py:26
  25.2 4.6 %collective-permute-done.3 = f32[12,20,2,128]{3,0,2,1:T(8,128)S(1)} collective-permute-done((f32[12,20,2,128]{3,0,2,1:T(8,128)S(1)}, f32[12,20,2,128]{3,0,2,1:T(8,128)S(1)}, u32[]{:S(2)}, u32[]{:S(2)}) %collective-permute-start.3) | collective-permute-done | bytes 245792 | tf_op jit(solution)/shard_map/ppermute | solution.py:27
  29.8 0.2 pad_maximum_fusion
  30.0 0.1 fusion.41
  30.1 2.3 %fusion.8 = f32[12,18,10,128]{3,0,2,1:T(8,128)S(1)} fusion(f32[12,20,12,128]{3,0,2,1:T(8,128)S(1)} %pad_maximum_fusion, f32[12,20,8,128]{3,0,2,1:T(8,128)S(1)} %constant_dynamic-update-slice_fusion, f32[12,20,2,128]{3,0,2,1:T(8,128)S(1)} %collective-permute-done.2, f32[12,20,2,128]{3,0,2,1:T(8,128)S(1)} %collective-permute-done.3, ...), kind=kOutput, calls=%fused_computation.14 | convolution fusion | flops 44236800 | bytes 11096576 | tf_op jit(solution)/shard_map/vw,wxyz->vxyz/dot_general | solution.py:48
  32.5 0.1 fusion.42
  32.6 2.2 %fusion.23 = f32[12,16,8,128]{3,0,2,1:T(8,128)S(1)} fusion(f32[12,18,10,128]{3,0,2,1:T(8,128)S(1)} %fusion.8, f32[16,8,128]{2,1,0:T(8,128)S(1)} %bitcast.62, f32[12]{0:T(128)S(1)} %neg.5, f32[12]{0:T(128)S(1)} %copy-done.8, f32[12]{0:T(128)S(1)} %copy-done.9, f32[12,16,8,128]{3,2,1,0:T(8,128)S(1)} %copy-done.2, f32[12,12]{1,0:T(8,128)S(1)} %copy-done.6), kind=kOutput, calls=%fused_computation.37 | convolution fusion | flops 31260672 | bytes 9414144 | tf_op jit(solution)/shard_map/vw,wxyz->vxyz/dot_general | solution.py:48
  34.8 0.0 copy-start.5
  34.8 1.0 fusion.44
  35.8 0.0 copy-done.5
  35.8 0.0 copy-start.3
  35.8 0.7 fusion.51
  36.5 0.5 copy.49
  37.1 0.0 copy-start.4
  37.1 1.7 convolution_bitcast_fusion.3
  38.7 1.1 copy.51
  39.8 0.0 reduce-scatter.2.cloned.1.call-update
  39.9 0.0 all-reduce.6.cloned.1.call-start
  39.9 27.8 %reduce-scatter.2.cloned.1.call-done = f32[16,8,192]{2,1,0:T(8,128)} async-done(((f32[64,8,192]{2,1,0:T(8,128)}), f32[16,8,192]{2,1,0:T(8,128)}) %reduce-scatter.2.cloned.1.call-update) | async-done | bytes 98320 | tf_op jit(solution)/shard_map/reduce_scatter | solution.py:87
  67.7 2.9 %convolution_bitcast_fusion.1 = f32[16,64,192]{2,1,0:T(8,128)} fusion(f32[16,8,192]{2,1,0:T(8,128)} %reduce-scatter.2.cloned.1.call-done, f32[8,64]{1,0:T(8,128)S(1)} %copy-done.4), kind=kOutput, calls=%fused_computation.23 | convolution fusion | flops 18874368 | bytes 886784 | tf_op jit(solution)/shard_map/ayk,yb->abk/dot_general | solution.py:93
  70.6 0.0 all-reduce.6.cloned.1.call-update
  70.6 1.1 copy.57
  71.7 77.8 %all-reduce.6.cloned.1.call-done = f32[16,64,192]{2,1,0:T(8,128)} async-done(((f32[16,64,192]{2,1,0:T(8,128)}), f32[16,64,192]{2,1,0:T(8,128)}) %all-reduce.6.cloned.1.call-update) | async-done | bytes 786448 | tf_op jit(solution)/shard_map/psum | solution.py:94
  149.5 1.9 convolution_bitcast_fusion.5
  151.3 7.3 %all_gather.3 = f32[64,8,192]{2,1,0:T(8,128)S(1)} all-gather(f32[16,8,192]{2,1,0:T(8,128)S(1)} %convolution_bitcast_fusion.5), channel_id=1, replica_groups=mesh['gx'=4,'gy'=8] {'gx'}, dimensions={0}, use_global_device_ids=true | all-gather | bytes 491520 | tf_op jit(solution)/shard_map/all_gather | solution.py:98
  158.7 0.5 convolution_bitcast_fusion.4
  159.2 0.3 copy.53
  159.5 0.6 copy.54
  160.1 1.0 convolution_bitcast_fusion
  161.2 0.9 fusion.31
  162.1 0.0 copy-start.1
  162.1 0.7 multiply_reduce_fusion
  162.8 20.0 %all-reduce.2 = (f32[12]{0:T(128)S(1)}, f32[12]{0:T(128)S(1)}) all-reduce(f32[12]{0:T(128)S(1)} %get-tuple-element.16, f32[12]{0:T(128)S(1)} %get-tuple-element.15), channel_id=1, replica_groups=mesh['gx'=4,'gy'=8] {'gy'}, use_global_device_ids=true, to_apply=%region_3.4 | all-reduce | flops 24 | bytes 192 | tf_op jit(solution)/shard_map/psum | solution.py:12
  182.8 5.6 %all-reduce.3 = (f32[12]{0:T(128)S(1)}, f32[12]{0:T(128)S(1)}) all-reduce(f32[12]{0:T(128)S(1)} %get-tuple-element.17, f32[12]{0:T(128)S(1)} %get-tuple-element.18), channel_id=1, replica_groups=mesh['gx'=4,'gy'=8] {'gx'}, use_global_device_ids=true, to_apply=%region_4.5 | all-reduce | flops 24 | bytes 192 | tf_op jit(solution)/shard_map/psum | solution.py:12
  188.5 0.5 fusion.55
  (21 shorter events, 0.2 us)
Async XLA Ops:
  7.2 27.6 %copy-start = (f32[128,32]{0,1:T(8,128)S(1)}, f32[128,32]{0,1:T(8,128)}, u32[]{:S(2)}) copy-start(f32[128,32]{0,1:T(8,128)} %param.16) | copy-start | bytes 49156
  7.2 4.9 %copy-start.2 = (f32[12,16,8,128]{3,2,1,0:T(8,128)S(1)}, f32[12,16,8,128]{3,2,1,0:T(8,128)}, u32[]{:S(2)}) copy-start(f32[12,16,8,128]{3,2,1,0:T(8,128)} %param.9) | copy-start | bytes 2359300
  7.2 60.5 %reduce-scatter.2.cloned.1.call-start = ((), (), s32[]{:S(2)}) async-start(), calls=%async_computation.1 | async-start | bytes 655360 | tf_op jit(solution)/shard_map/reduce_scatter | solution.py:87
  8.3 3.8 %collective-permute-start = (f32[12,2,8,128]{3,0,2,1:T(8,128)S(1)}, f32[12,2,8,128]{3,0,2,1:T(8,128)S(1)}, u32[]{:S(2)}, u32[]{:S(2)}) collective-permute-start(f32[12,2,8,128]{3,0,2,1:T(8,128)S(1)} %copy.76), channel_id=1, source_target_pairs={{0,8},{8,16},{16,24},{1,9},{9,17},{17,25},{2,10},{10,18},{18,26},{... | collective-permute-start | bytes 294920 | tf_op jit(solution)/shard_map/ppermute | solution.py:26
  10.8 5.3 %collective-permute-start.1 = (f32[12,2,8,128]{3,0,2,1:T(8,128)S(1)}, f32[12,2,8,128]{3,0,2,1:T(8,128)S(1)}, u32[]{:S(2)}, u32[]{:S(2)}) collective-permute-start(f32[12,2,8,128]{3,0,2,1:T(8,128)S(1)} %copy.77), channel_id=1, source_target_pairs={{8,0},{16,8},{24,16},{9,1},{17,9},{25,17},{10,2},{18,10},{26,18},{... | collective-permute-start | bytes 294920 | tf_op jit(solution)/shard_map/ppermute | solution.py:27
  12.1 8.8 %copy-start.7 = (f32[12]{0:T(128)S(1)}, f32[12]{0:T(128)}, u32[]{:S(2)}) copy-start(f32[12]{0:T(128)} %param.12) | copy-start | bytes 148
  16.2 9.0 %collective-permute-start.2 = (f32[12,20,2,128]{3,0,2,1:T(8,128)S(1)}, f32[12,20,2,128]{3,0,2,1:T(8,128)S(1)}, u32[]{:S(2)}, u32[]{:S(2)}) collective-permute-start(f32[12,20,2,128]{3,0,2,1:T(8,128)S(1)} %get-tuple-element.21), channel_id=1, source_target_pairs={{0,1},{1,2},{2,3},{3,4},{4,5},{5,6},{6,7},{8,9},{9,10},{10,11},{11... | collective-permute-start | bytes 737288 | tf_op jit(solution)/shard_map/ppermute | solution.py:26
  19.6 10.2 %collective-permute-start.3 = (f32[12,20,2,128]{3,0,2,1:T(8,128)S(1)}, f32[12,20,2,128]{3,0,2,1:T(8,128)S(1)}, u32[]{:S(2)}, u32[]{:S(2)}) collective-permute-start(f32[12,20,2,128]{3,0,2,1:T(8,128)S(1)} %get-tuple-element.22), channel_id=1, source_target_pairs={{1,0},{2,1},{3,2},{4,3},{5,4},{6,5},{7,6},{9,8},{10,9},{11,10},{12... | collective-permute-start | bytes 737288 | tf_op jit(solution)/shard_map/ppermute | solution.py:27
  21.0 9.1 %copy-start.6 = (f32[12,12]{1,0:T(8,128)S(1)}, f32[12,12]{1,0:T(8,128)}, u32[]{:S(2)}) copy-start(f32[12,12]{1,0:T(8,128)} %param.13) | copy-start | bytes 1732
  21.0 9.1 %copy-start.8 = (f32[12]{0:T(128)S(1)}, f32[12]{0:T(128)}, u32[]{:S(2)}) copy-start(f32[12]{0:T(128)} %param.11) | copy-start | bytes 148
  21.0 9.1 %copy-start.9 = (f32[12]{0:T(128)S(1)}, f32[12]{0:T(128)}, u32[]{:S(2)}) copy-start(f32[12]{0:T(128)} %param.10) | copy-start | bytes 148
  34.8 1.0 copy-start.5
  35.8 1.3 copy-start.3
  37.1 30.6 %copy-start.4 = (f32[8,64]{1,0:T(8,128)S(1)}, f32[8,64]{1,0:T(8,128)}, u32[]{:S(2)}) copy-start(f32[8,64]{1,0:T(8,128)} %param.15) | copy-start | bytes 6148
  39.9 109.6 %all-reduce.6.cloned.1.call-start = ((), (), s32[]{:S(2)}) async-start(), calls=%async_computation.2 | async-start | bytes 2097152 | tf_op jit(solution)/shard_map/psum | solution.py:94
  162.1 26.9 %copy-start.1 = (f32[12,16,8,128]{3,2,1,0:T(8,128)}, f32[12,16,8,128]{3,2,1,0:T(8,128)S(1)}, u32[]{:S(2)}) copy-start(f32[12,16,8,128]{3,2,1,0:T(8,128)S(1)} %fusion.31) | copy-start | bytes 2359300
Sparse Core Ops, SparseCore 0:
  40.0 27.6 reduce-scatter.1
  71.2 78.2 all-reduce.5
